TPU v7x, 256 devices: a whole 4x4x8 slice. The times are simulated.
256 devices in a mesh: replica: 32 (over x, z), tensor: 8 (over y, core).
Axes of the slice: x: 4, y: 4, z: 8, core: 2. Of those that a mesh axis runs over, the one named last changes fastest.
Arguments:
- tokens: bfloat16 [96, 2048], P('replica'), may hold values from -0.8984375 to 0.8984375
- long_tokens: bfloat16 [32, 2048], P('replica'), may hold values from -0.8984375 to 0.8984375
- cache: bfloat16 [2, 2, 96, 2048, 8, 128], P(None, None, 'replica', None, 'tensor')
- long_request_cache: bfloat16 [2, 2, 32, 2, 2048, 8, 128], P(None, None, 'replica', None, None, 'tensor')
- lengths: int32 [96], replicated, may hold values from 1 to 2047, as said below
- long_lengths: int32 [32], replicated, may hold values from 2049 to 4095, as said below
- norm_gain: float32 [2, 2048], replicated, may hold values from 0.1 to 1.9
- q_gain: float32 [2, 128], replicated, may hold values from 0.1 to 1.9
- k_gain: float32 [2, 128], replicated, may hold values from 0.1 to 1.9
- w_query: bfloat16 [2, 2048, 2048], P(None, None, 'tensor'), may hold values from -0.125 to 0.125
- key_weight: bfloat16 [2, 2048, 1024], P(None, None, 'tensor'), may hold values from -0.125 to 0.125
- value_weight: bfloat16 [2, 2048, 1024], P(None, None, 'tensor'), may hold values from -0.125 to 0.125
- w_out: bfloat16 [2, 2048, 2048], P(None, 'tensor'), may hold values from -0.125 to 0.125
Outputs:
- out_hidden: float32 [96, 2048], P('replica')
- out_long: float32 [32, 2048], P('replica')
- moved_cache: bfloat16 [32, 2, 2, 2048, 8, 128], P('replica', None, None, None, 'tensor')
Inputs may be any that keep to these rules, and one draw needn't show every extreme that they name: `lengths`: cached length of each request; some request has 2047 in every draw. `long_lengths`: cached length of each long request, always past 2048; some long request has 4095 in every draw.
All inputs are finite; a program needn't handle non-finite values.
Results may differ from a plain program's by a relative error of at most 0.028.
Values may be sent and summed in bfloat16 or wider, within the bound.
No kernel may reach another device: no remote copies, remote signals or barrier semaphores. Data moves between devices by JAX's collectives and lax.ppermute only.
A program may use at most 64 MiB of HBM per device.

v0:
```python
import jax
import jax.numpy as jnp
from jax import lax
from jax.sharding import PartitionSpec as P

EPSILON = 1e-06
ROPE_BASE = 1000000.0
NEGATIVE = -1e30


def shifted(block, axis, distance):
    devices = range(lax.axis_size(axis))
    route = [((i - distance) % len(devices), i) for i in devices]
    return lax.ppermute(block, axis, route)


def partner_2(value, axis, apart):
    mask = 2**apart
    pairs = [(source, source ^ mask) for source in range(lax.axis_size(axis))]
    return lax.ppermute(value, axis, pairs)


def rms_scale(values, gain_row):
    return (
        values * lax.rsqrt(jnp.mean(values * values, axis=-1, keepdims=True) + EPSILON) * gain_row
    )


def rotate(values, places):
    head_width = values.shape[-1]
    halfway = head_width // 2
    inverse = ROPE_BASE ** (-2.0 * jnp.arange(halfway, dtype=jnp.float32) / head_width)
    angles = places.astype(jnp.float32)[:, None, None] * inverse
    cosine = jnp.cos(angles)
    sine_of = jnp.sin(angles)
    leading = values[..., :halfway]
    trailing = values[..., halfway:]
    return jnp.concatenate(
        [leading * cosine - trailing * sine_of, trailing * cosine + leading * sine_of], axis=-1
    )


def project(hidden, gain_row, w_query, key_weight, value_weight, query_gain, key_gain, places):
    head_width = query_gain.shape[-1]
    count_rows = hidden.shape[0]
    normed = rms_scale(hidden.astype(jnp.float32), gain_row).astype(jnp.bfloat16)
    queries = jnp.dot(normed, w_query, preferred_element_type=jnp.float32).reshape(
        count_rows, -1, head_width
    )
    keys_new = jnp.dot(normed, key_weight, preferred_element_type=jnp.float32).reshape(
        count_rows, -1, head_width
    )
    values_new = (
        jnp.dot(normed, value_weight, preferred_element_type=jnp.float32)
        .reshape(count_rows, -1, head_width)
        .astype(jnp.bfloat16)
    )
    queries = rotate(rms_scale(queries, query_gain), places).astype(jnp.bfloat16)
    keys_new = rotate(rms_scale(keys_new, key_gain), places).astype(jnp.bfloat16)
    return (queries, keys_new, values_new)


def own_terms(queries, key_new):
    head_width = queries.shape[-1]
    grouped = queries.reshape(key_new.shape[0], -1, head_width)
    return jnp.einsum(
        "kgd,kd->kg", grouped, key_new, preferred_element_type=jnp.float32
    ) * head_width ** (-0.5)


def masked_scores(queries, key_rows, visible):
    head_width = queries.shape[-1]
    grouped = queries.reshape(key_rows.shape[1], -1, head_width)
    scores = jnp.einsum(
        "kgd,tkd->kgt", grouped, key_rows, preferred_element_type=jnp.float32
    ) * head_width ** (-0.5)
    return jnp.where(visible[None, None, :], scores, NEGATIVE)


def attend(queries, key_rows, value_rows, visible, key_new, value_new):
    scores = masked_scores(queries, key_rows, visible)
    own_score = own_terms(queries, key_new)
    highest = jnp.maximum(jnp.max(scores, axis=-1), own_score)
    weights = jnp.exp(scores - highest[..., None])
    own_weight = jnp.exp(own_score - highest)
    denominator = jnp.sum(weights, axis=-1) + own_weight
    summed = jnp.einsum(
        "kgt,tkd->kgd", weights.astype(jnp.bfloat16), value_rows, preferred_element_type=jnp.float32
    )
    own_rounded = lax.optimization_barrier(own_weight.astype(jnp.bfloat16)).astype(jnp.float32)
    summed = summed + own_rounded[..., None] * value_new.astype(jnp.float32)[:, None, :]
    return (summed / denominator[..., None]).reshape(queries.shape).astype(jnp.bfloat16)


def partial_attend(queries, key_rows, value_rows, visible):
    scores = masked_scores(queries, key_rows, visible)
    highest = jnp.max(scores, axis=-1)
    weights = jnp.exp(scores - highest[..., None])
    summed = jnp.einsum(
        "kgt,tkd->kgd", weights.astype(jnp.bfloat16), value_rows, preferred_element_type=jnp.float32
    )
    return (highest, jnp.sum(weights, axis=-1), summed)


def combine(one_side, far_side):
    highest = jnp.maximum(one_side[0], far_side[0])
    factor_here = jnp.exp(one_side[0] - highest)
    factor_far = jnp.exp(far_side[0] - highest)
    totals = one_side[1] * factor_here + far_side[1] * factor_far
    summed = one_side[2] * factor_here[..., None] + far_side[2] * factor_far[..., None]
    return (highest, totals, summed)


def close_with_own(state_in, queries, key_new, value_new):
    own_score = own_terms(queries, key_new)
    highest = jnp.maximum(state_in[0], own_score)
    factor_here = jnp.exp(state_in[0] - highest)
    own_weight = jnp.exp(own_score - highest)
    denominator = state_in[1] * factor_here + own_weight
    own_rounded = lax.optimization_barrier(own_weight.astype(jnp.bfloat16)).astype(jnp.float32)
    summed = (
        state_in[2] * factor_here[..., None]
        + own_rounded[..., None] * value_new.astype(jnp.float32)[:, None, :]
    )
    return (summed / denominator[..., None]).reshape(queries.shape).astype(jnp.bfloat16)


def local(
    tokens,
    long_tokens,
    cache,
    long_request_cache,
    lengths,
    long_lengths,
    norm_gain,
    q_gain,
    k_gain,
    w_query,
    key_weight,
    value_weight,
    w_out,
):
    groups = lax.axis_size("replica")
    group_at = lax.axis_index("replica")
    per_group = tokens.shape[0]
    resident = per_group - 1
    layers = cache.shape[0]
    positions = jnp.arange(cache.shape[3])
    half_len = long_request_cache.shape[4]
    partner = (group_at + groups // 2) % groups
    local_len = lax.dynamic_slice_in_dim(lengths, group_at * per_group, per_group)
    arrived_len = lax.dynamic_index_in_dim(
        lengths, partner * per_group + resident, 0, keepdims=False
    )
    parity = group_at % 2
    pair_len = lax.dynamic_slice_in_dim(long_lengths, group_at - parity, 2)
    arrived_cache, arrived_token = shifted(
        (cache[:, :, resident], tokens[resident:]), "replica", groups // 2
    )
    hidden = jnp.concatenate([tokens[:resident], arrived_token], axis=0)
    places = jnp.concatenate([local_len[:resident], arrived_len[None]])
    visible = positions[None, :] < places[:, None]
    partner_token = partner_2(long_tokens, "replica", 0)
    long_hidden = jnp.where(
        parity == 0,
        jnp.concatenate([long_tokens, partner_token], axis=0),
        jnp.concatenate([partner_token, long_tokens], axis=0),
    )
    offsets = parity * half_len + jnp.arange(half_len)
    long_visible = offsets[None, :] < pair_len[:, None]
    main_rows = hidden.shape[0]
    fresh_rows = []
    for layer_at in range(layers):
        queries, keys_new, values_new = project(
            hidden,
            norm_gain[layer_at],
            w_query[layer_at],
            key_weight[layer_at],
            value_weight[layer_at],
            q_gain[layer_at],
            k_gain[layer_at],
            places,
        )
        staying = jax.vmap(attend)(
            queries[:resident],
            cache[layer_at, 0, :resident],
            cache[layer_at, 1, :resident],
            visible[:resident],
            keys_new[:resident],
            values_new[:resident],
        )
        incoming = attend(
            queries[resident],
            arrived_cache[layer_at, 0],
            arrived_cache[layer_at, 1],
            visible[resident],
            keys_new[resident],
            values_new[resident],
        )
        attended = jnp.concatenate([staying, incoming[None]], axis=0)
        fresh_rows.append(jnp.stack([keys_new[resident], values_new[resident]]))
        long_queries, long_keys, long_values = project(
            long_hidden,
            norm_gain[layer_at],
            w_query[layer_at],
            key_weight[layer_at],
            value_weight[layer_at],
            q_gain[layer_at],
            k_gain[layer_at],
            pair_len,
        )
        state_here = jax.vmap(partial_attend)(
            long_queries,
            long_request_cache[layer_at, 0, 0],
            long_request_cache[layer_at, 1, 0],
            long_visible,
        )
        state_far = partner_2(state_here, "replica", 0)
        merged = combine(state_here, state_far)
        long_attended = jax.vmap(close_with_own)(merged, long_queries, long_keys, long_values)
        stacked = jnp.concatenate([attended, long_attended], axis=0)
        heads_out = jnp.dot(
            stacked.reshape(stacked.shape[0], -1),
            w_out[layer_at],
            preferred_element_type=jnp.float32,
        )
        summed = lax.psum(heads_out, "tensor")
        carried = jnp.concatenate([hidden, long_hidden], axis=0).astype(jnp.float32) + summed
        if layer_at + 1 < layers:
            carried = carried.astype(jnp.bfloat16)
        hidden = carried[:main_rows]
        long_hidden = carried[main_rows:]
    fresh_all = jnp.stack(fresh_rows)
    moved_here = lax.dynamic_update_slice_in_dim(
        arrived_cache, fresh_all[:, :, None], arrived_len, axis=2
    )
    long_out = lax.dynamic_slice_in_dim(long_hidden, parity, 1)
    return (hidden, long_out, moved_here[None])


def solution(mesh):
    return jax.shard_map(
        local,
        mesh=mesh,
        in_specs=(
            P("replica", None),
            P("replica", None),
            P(None, None, "replica", None, "tensor", None),
            P(None, None, "replica", None, None, "tensor", None),
            P(),
            P(),
            P(),
            P(),
            P(),
            P(None, None, "tensor"),
            P(None, None, "tensor"),
            P(None, None, "tensor"),
            P(None, "tensor", None),
        ),
        out_specs=(
            P("replica", None),
            P("replica", None),
            P("replica", None, None, None, "tensor", None),
        ),
        check_vma=False,
    )
```

profile of v0, /device:TPU:64, one launch (start us, length us, event | category | flops | bytes accessed | tf_op | source)
XLA Modules:
  0.0 137.5 jit_solution(526159633632751661)
XLA Ops:
  0.6 0.7 slice.220
  1.4 3.1 %collective-permute-start = (bf16[1,2048]{1,0:T(2,128)(2,1)S(1)}, bf16[1,2048]{1,0:T(2,128)(2,1)S(1)}, u32[]{:S(2)}, u32[]{:S(2)}) collective-permute-start(bf16[1,2048]{1,0:T(2,128)(2,1)S(1)} %slice.220), channel_id=1, source_target_pairs={{128,0},{136,8},{144,16},{152,24},{160,32},{168,40},{176,48},{184,... | collective-permute-start | bytes 12296 | tf_op jit(solution)/shard_map/ppermute | solution.py:14
  4.5 1.9 %collective-permute-start.1 = (bf16[1,2048]{1,0:T(2,128)(2,1)}, bf16[1,2048]{1,0:T(2,128)(2,1)S(1)}, u32[]{:S(2)}, u32[]{:S(2)}) collective-permute-start(bf16[1,2048]{1,0:T(2,128)(2,1)} %param.14), channel_id=1, source_target_pairs={{0,8},{8,0},{16,24},{24,16},{32,40},{40,32},{48,56},{56,48},{64,72... | collective-permute-start | bytes 12296 | tf_op jit(solution)/shard_map/ppermute | solution.py:20
  6.5 3.0 %slice_bitcast_fusion = bf16[2,2,2048,1,128]{4,2,1,0,3:T(8,128)(2,1)} fusion(bf16[2,2,3,2048,1,128]{5,3,4,2,1,0:T(8,128)(2,1)} %param.15), kind=kLoop, calls=%fused_computation.12 | loop fusion | bytes 4194304 | tf_op jit(solution)/shard_map/squeeze | solution.py:158
  9.5 0.5 collective-permute-start.2
  10.0 0.6 dynamic_slice.14
  10.7 0.7 fusion.200
  11.9 1.7 %slice_bitcast_fusion.18 = (bf16[256,2048]{0,1:T(8,128)(2,1)S(1)}, bf16[256,2048]{0,1:T(8,128)(2,1)S(1)}) fusion(bf16[2,2048,256]{2,1,0:T(8,128)(2,1)} %param.22), kind=kLoop, calls=%fused_computation.56 | loop fusion | bytes 4194304 | tf_op jit(solution)/shard_map/dot_general | solution.py:47
  15.0 0.6 copy.34
  15.7 0.6 copy.42
  17.2 1.4 %multiply_reduce_fusion.5 = (f32[3]{0:T(128)S(1)}, f32[3,128]{1,0:T(4,128)S(1)}) fusion(bf16[2,2048,128]{2,1,0:T(8,128)(2,1)} %param.23, f32[2048]{0:T(1024)S(1)} %bitcast.414, f32[3]{0:T(128)S(1)} %add_rsqrt_fusion.11, bf16[1,2048]{1,0:T(2,128)(2,1)S(1)} %collective-permute-done, bf16[2,2048]{1,0:T(2,128)(2,1)S(1)} %slice.219), kind=kOutput, calls=%fused_computation.200 | convolution fusion | flops 1616637 | bytes 546328 | tf_op jit(solution)/shard_map/dot_general | solution.py:50
  19.0 1.4 %multiply_reduce_fusion.7 = (f32[2]{0:T(128)S(1)}, f32[2,128]{1,0:T(2,128)S(1)}) fusion(bf16[2,2048,128]{2,1,0:T(8,128)(2,1)} %param.23, bf16[2,2048]{1,0:T(2,128)(2,1)S(1)} %get-tuple-element.12, f32[2]{0:T(128)S(1)} %add_rsqrt_fusion.9, f32[2048]{0:T(1024)S(1)} %bitcast.415), kind=kOutput, calls=%fused_computation.252 | convolution fusion | flops 1065470 | bytes 541712 | tf_op jit(solution)/shard_map/dot_general | solution.py:50
  20.4 0.5 multiply_reduce_fusion.4
  21.1 1.7 %fusion.203 = (f32[2,2]{1,0:T(2,128)S(1)}, f32[2,2,2048]{2,1,0:T(2,128)S(1)}) fusion(bf16[2,2,1,2,2048,1,128]{6,4,3,5,2,1,0:T(8,128)(2,1)} %bitcast.441, bf16[2,2,128]{2,0,1:T(2,128)(2,1)S(1)} %pad_maximum_fusion.4, pred[2,2048]{1,0:T(4,128)(4,1)S(1)} %broadcast_compare_fusion), kind=kOutput, calls=%fused_computation.350 | convolution fusion | flops 2121724 | bytes 1086480 | tf_op jit(solution)/shard_map/vmap(kgd,tkd->kgt)/dot_general | solution.py:74
  23.0 1.5 %fusion.23 = f32[2,2,128]{2,1,0:T(2,128)S(1)} fusion(bf16[2,2,1,2,2048,1,128]{6,4,3,5,2,1,0:T(8,128)(2,1)} %bitcast.442, f32[2,2,2048]{2,1,0:T(2,128)S(1)} %get-tuple-element.64, f32[2,2]{1,0:T(2,128)S(1)} %get-tuple-element.63), kind=kOutput, calls=%fused_computation.45 | convolution fusion | flops 2113536 | bytes 1083408 | tf_op jit(solution)/shard_map/vmap(kgt,tkd->kgd)/dot_general | solution.py:99
  24.8 0.5 multiply_reduce_fusion.1
  25.7 1.8 %fusion.205 = (f32[2,2]{1,0:T(2,128)S(1)}, f32[2,2,2048]{2,1,0:T(2,128)S(1)}) fusion(bf16[2,2,3,2048,1,128]{5,3,2,4,1,0:T(8,128)(2,1)} %bitcast.404, bf16[2,2,128]{2,0,1:T(2,128)(2,1)S(1)} %fusion.143, pred[2,2048]{1,0:T(4,128)(4,1)S(1)} %bitcast.420), kind=kOutput, calls=%fused_computation.352 | convolution fusion | flops 2121724 | bytes 1086480 | tf_op jit(solution)/shard_map/vmap(kgd,tkd->kgt)/dot_general | solution.py:74
  27.7 1.5 %fusion.11 = bf16[1,2,2,128]{3,2,1,0:T(2,128)(2,1)S(1)} fusion(bf16[2,2,3,2048,1,128]{5,3,2,4,1,0:T(8,128)(2,1)} %bitcast.405, f32[2,2,2048]{2,1,0:T(2,128)S(1)} %get-tuple-element.72, f32[2,2]{1,0:T(2,128)S(1)} %multiply_maximum_fusion.1, f32[2,2]{1,0:T(2,128)S(1)} %get-tuple-element.42, f32[2,128]{1,0:T(2,128)S(1)} %slice_convert_fusion.1, ...), kind=kOutput, calls=%fused_computation.22 | convolution fusion | flops 2115584 | bytes 1083440 | tf_op jit(solution)/shard_map/vmap(kgt,tkd->kgd)/dot_general | solution.py:87
  29.5 1.9 %collective-permute-start.3 = (f32[2,1,2]{2,0,1:T(2,128)S(1)}, f32[2,1,2]{2,0,1:T(2,128)S(1)}, u32[]{:S(2)}, u32[]{:S(2)}) collective-permute-start(f32[2,1,2]{2,0,1:T(2,128)S(1)} %bitcast.428), channel_id=1, source_target_pairs={{0,8},{8,0},{16,24},{24,16},{32,40},{40,32},{48,56},{56,48},{64,72... | collective-permute-start | bytes 56 | tf_op jit(solution)/shard_map/ppermute | solution.py:20
  32.3 0.6 collective-permute-done.5
  33.1 1.9 %collective-permute-done.4 = f32[2,1,2,128]{3,2,0,1:T(2,128)S(1)} collective-permute-done((f32[2,1,2,128]{3,2,0,1:T(2,128)S(1)}, f32[2,1,2,128]{3,2,0,1:T(2,128)S(1)}, u32[]{:S(2)}, u32[]{:S(2)}) %collective-permute-start.4) | collective-permute-done | bytes 2080 | tf_op jit(solution)/shard_map/ppermute | solution.py:20
  35.1 23.1 %collective-permute-done.2 = bf16[2,2,2048,1,128]{4,2,1,0,3:T(8,128)(2,1)} collective-permute-done((bf16[2,2,2048,1,128]{4,2,1,0,3:T(8,128)(2,1)}, bf16[2,2,2048,1,128]{4,2,1,0,3:T(8,128)(2,1)}, u32[]{:S(2)}, u32[]{:S(2)}) %collective-permute-start.2) | collective-permute-done | bytes 2097184 | tf_op jit(solution)/shard_map/ppermute | solution.py:14
  58.1 1.4 %fusion.204 = (f32[2]{0:T(128)S(1)}, f32[2,2048]{1,0:T(2,128)S(1)}) fusion(bf16[2,2,2048,1,128]{4,2,1,0,3:T(8,128)(2,1)} %collective-permute-done.2, bf16[1,2,128]{2,0,1:T(2,128)(2,1)S(1)} %pad_maximum_fusion.2, pred[2048]{0:T(1024)(128)(4,1)S(1)} %slice_reduce_fusion), kind=kOutput, calls=%fused_computation.351 | convolution fusion | flops 1060862 | bytes 543240 | tf_op jit(solution)/shard_map/kgd,tkd->kgt/dot_general | solution.py:74
  59.8 1.3 fusion.19
  61.3 24.8 %psum.14 = f32[5,2048]{1,0:T(8,128)S(1)} all-reduce(f32[5,2048]{1,0:T(8,128)S(1)} %fusion.26), channel_id=1, replica_groups=mesh['replica'=32,'tensor'=8] {'tensor'}, use_global_device_ids=true, to_apply=%region_12.13 | all-reduce | flops 10240 | bytes 81920 | tf_op jit(solution)/shard_map/psum | solution.py:227
  86.5 1.4 %convolution_convert_fusion = bf16[3,128]{1,0:T(4,128)(2,1)S(1)} fusion(bf16[2,2048,128]{2,1,0:T(8,128)(2,1)} %param.24, f32[2048]{0:T(1024)S(1)} %bitcast.408, f32[3]{0:T(128)S(1)} %add_rsqrt_fusion.7, bf16[5,2048]{1,0:T(8,128)(2,1)S(1)} %add_convert_fusion), kind=kOutput, calls=%fused_computation.17 | convolution fusion | flops 1597824 | bytes 550144 | tf_op jit(solution)/shard_map/dot_general | solution.py:54
  87.9 1.3 fusion.16
  89.2 1.4 %multiply_reduce_fusion.6 = (f32[2]{0:T(128)S(1)}, f32[2,128]{1,0:T(2,128)S(1)}) fusion(bf16[2,2048,128]{2,1,0:T(8,128)(2,1)} %param.23, f32[2]{0:T(128)S(1)} %add_rsqrt_fusion.5, f32[2048]{0:T(1024)S(1)} %bitcast.410, bf16[5,2048]{1,0:T(8,128)(2,1)S(1)} %add_convert_fusion), kind=kOutput, calls=%fused_computation.244 | convolution fusion | flops 1065470 | bytes 542216 | tf_op jit(solution)/shard_map/dot_general | solution.py:50
  90.6 0.5 multiply_reduce_fusion.2
  91.1 0.5 multiply_reduce_fusion
  91.5 1.4 %multiply_reduce_fusion.3 = (f32[3]{0:T(128)S(1)}, f32[3,128]{1,0:T(4,128)S(1)}) fusion(bf16[2,2048,128]{2,1,0:T(8,128)(2,1)} %param.23, f32[2048]{0:T(1024)S(1)} %bitcast.413, f32[3]{0:T(128)S(1)} %add_rsqrt_fusion.7, bf16[5,2048]{1,0:T(8,128)(2,1)S(1)} %add_convert_fusion), kind=kOutput, calls=%fused_computation.194 | convolution fusion | flops 1598205 | bytes 550924 | tf_op jit(solution)/shard_map/dot_general | solution.py:50
  93.8 0.5 fusion.206
  94.5 0.3 fusion.22
  95.3 1.7 %fusion.208 = (f32[2,2]{1,0:T(2,128)S(1)}, f32[2,2,2048]{2,1,0:T(2,128)S(1)}) fusion(bf16[2,2,3,2048,1,128]{5,3,2,4,1,0:T(8,128)(2,1)} %bitcast.406, bf16[2,2,128]{2,0,1:T(2,128)(2,1)S(1)} %fusion.142, pred[2,2048]{1,0:T(4,128)(4,1)S(1)} %bitcast.421), kind=kOutput, calls=%fused_computation.355 | convolution fusion | flops 2121724 | bytes 1086480 | tf_op jit(solution)/shard_map/vmap(kgd,tkd->kgt)/dot_general | solution.py:74
  97.2 1.4 %fusion.207 = (f32[2]{0:T(128)S(1)}, f32[2,2048]{1,0:T(2,128)S(1)}) fusion(bf16[2,2,2048,1,128]{4,2,1,0,3:T(8,128)(2,1)} %collective-permute-done.2, bf16[1,2,128]{2,0,1:T(2,128)(2,1)S(1)} %pad_maximum_fusion.1, pred[2048]{0:T(1024)(128)(4,1)S(1)} %slice_reduce_fusion), kind=kOutput, calls=%fused_computation.354 | convolution fusion | flops 1060862 | bytes 543240 | tf_op jit(solution)/shard_map/kgd,tkd->kgt/dot_general | solution.py:74
  98.8 1.3 fusion.18
  100.1 1.3 dynamic_update_slice.4
  101.7 1.5 %fusion.10 = bf16[1,2,2,128]{3,2,1,0:T(2,128)(2,1)S(1)} fusion(bf16[2,2,3,2048,1,128]{5,3,2,4,1,0:T(8,128)(2,1)} %bitcast.407, f32[2,2,2048]{2,1,0:T(2,128)S(1)} %get-tuple-element.86, f32[2,2]{1,0:T(2,128)S(1)} %multiply_maximum_fusion, f32[2,2]{1,0:T(2,128)S(1)} %get-tuple-element.36, f32[2,128]{1,0:T(2,128)S(1)} %slice_convert_fusion, ...), kind=kOutput, calls=%fused_computation.21 | convolution fusion | flops 2115584 | bytes 1083440 | tf_op jit(solution)/shard_map/vmap(kgt,tkd->kgd)/dot_general | solution.py:87
  103.2 0.5 collective-permute-start.8
  103.7 1.6 %collective-permute-start.6 = (f32[2,1,2]{2,0,1:T(2,128)S(1)}, f32[2,1,2]{2,0,1:T(2,128)S(1)}, u32[]{:S(2)}, u32[]{:S(2)}) collective-permute-start(f32[2,1,2]{2,0,1:T(2,128)S(1)} %bitcast.426), channel_id=1, source_target_pairs={{0,8},{8,0},{16,24},{24,16},{32,40},{40,32},{48,56},{56,48},{64,72... | collective-permute-start | bytes 56 | tf_op jit(solution)/shard_map/ppermute | solution.py:20
  105.3 0.4 collective-permute-start.7
  105.8 1.1 collective-permute-done.8
  106.9 0.4 collective-permute-done.6
  107.3 1.6 %collective-permute-done.7 = f32[2,1,2,128]{3,2,0,1:T(2,128)S(1)} collective-permute-done((f32[2,1,2,128]{3,2,0,1:T(2,128)S(1)}, f32[2,1,2,128]{3,2,0,1:T(2,128)S(1)}, u32[]{:S(2)}, u32[]{:S(2)}) %collective-permute-start.7) | collective-permute-done | bytes 2080 | tf_op jit(solution)/shard_map/ppermute | solution.py:20
  109.3 23.9 %psum.15 = f32[5,2048]{1,0:T(8,128)S(1)} all-reduce(f32[5,2048]{1,0:T(8,128)S(1)} %fusion.24), channel_id=1, replica_groups=mesh['replica'=32,'tensor'=8] {'tensor'}, use_global_device_ids=true, to_apply=%region_25.26 | all-reduce | flops 10240 | bytes 81920 | tf_op jit(solution)/shard_map/psum | solution.py:227
  133.2 0.6 slice.313
  133.9 0.6 constant_dynamic-slice_fusion
  134.5 3.0 %copy.125 = bf16[1,2,2,2048,1,128]{5,3,4,2,1,0:T(8,128)(2,1)} copy(bf16[1,2,2,2048,1,128]{5,3,4,2,1,0:T(8,128)(2,1)} %dynamic_update_slice.4) | data formatting | bytes 4194304
  (134 shorter events, 7.3 us)
Async XLA Ops:
  1.4 8.7 %copy-start.9 = (s32[96]{0:T(128)S(1)}, s32[96]{0:T(128)}, u32[]{:S(2)}) copy-start(s32[96]{0:T(128)} %param.17) | copy-start | bytes 1156
  1.4 9.3 %copy-start.4 = (f32[2,128]{1,0:T(2,128)S(1)}, f32[2,128]{1,0:T(2,128)}, u32[]{:S(2)}) copy-start(f32[2,128]{1,0:T(2,128)} %param.20) | copy-start | bytes 3076
  1.4 9.3 %copy-start.5 = (f32[2,128]{1,0:T(2,128)S(1)}, f32[2,128]{1,0:T(2,128)}, u32[]{:S(2)}) copy-start(f32[2,128]{1,0:T(2,128)} %param.21) | copy-start | bytes 3076
  1.4 10.0 %copy-start.6 = (s32[32]{0:T(128)S(1)}, s32[32]{0:T(128)}, u32[]{:S(2)}) copy-start(s32[32]{0:T(128)} %param.18) | copy-start | bytes 388
  1.4 10.4 %copy-start.1 = (f32[2,2048]{1,0:T(2,128)S(1)}, f32[2,2048]{1,0:T(2,128)}, u32[]{:S(2)}) copy-start(f32[2,2048]{1,0:T(2,128)} %param.19) | copy-start | bytes 49156
  1.4 15.6 %collective-permute-start = (bf16[1,2048]{1,0:T(2,128)(2,1)S(1)}, bf16[1,2048]{1,0:T(2,128)(2,1)S(1)}, u32[]{:S(2)}, u32[]{:S(2)}) collective-permute-start(bf16[1,2048]{1,0:T(2,128)(2,1)S(1)} %slice.220), channel_id=1, source_target_pairs={{128,0},{136,8},{144,16},{152,24},{160,32},{168,40},{176,48},{184,... | collective-permute-start | bytes 12296 | tf_op jit(solution)/shard_map/ppermute | solution.py:14
  4.5 14.3 %collective-permute-start.1 = (bf16[1,2048]{1,0:T(2,128)(2,1)}, bf16[1,2048]{1,0:T(2,128)(2,1)S(1)}, u32[]{:S(2)}, u32[]{:S(2)}) collective-permute-start(bf16[1,2048]{1,0:T(2,128)(2,1)} %param.14), channel_id=1, source_target_pairs={{0,8},{8,0},{16,24},{24,16},{32,40},{40,32},{48,56},{56,48},{64,72... | collective-permute-start | bytes 12296 | tf_op jit(solution)/shard_map/ppermute | solution.py:20
  9.5 48.6 %collective-permute-start.2 = (bf16[2,2,2048,1,128]{4,2,1,0,3:T(8,128)(2,1)}, bf16[2,2,2048,1,128]{4,2,1,0,3:T(8,128)(2,1)}, u32[]{:S(2)}, u32[]{:S(2)}) collective-permute-start(bf16[2,2,2048,1,128]{4,2,1,0,3:T(8,128)(2,1)} %slice_bitcast_fusion), channel_id=1, source_target_pairs={{128,0},{136,8},{144,16},{152,24},{160,32},{168,40},{176,48},{184,... | collective-permute-start | bytes 6291464 | tf_op jit(solution)/shard_map/ppermute | solution.py:14
  11.9 3.1 %copy-start.2 = (bf16[3,2048]{1,0:T(4,128)(2,1)S(1)}, bf16[3,2048]{1,0:T(4,128)(2,1)}, u32[]{:S(2)}) copy-start(bf16[3,2048]{1,0:T(4,128)(2,1)} %param.13) | copy-start | bytes 36868
  15.0 3.8 %copy-start.3 = (bf16[1,2048]{1,0:T(2,128)(2,1)S(1)}, bf16[1,2048]{1,0:T(2,128)(2,1)}, u32[]{:S(2)}) copy-start(bf16[1,2048]{1,0:T(2,128)(2,1)} %param.14) | copy-start | bytes 12292
  18.5 6.0 %copy-start.8 = (bf16[2,2048,128]{2,1,0:T(8,128)(2,1)S(1)}, bf16[2,2048,128]{2,1,0:T(8,128)(2,1)}, u32[]{:S(2)}) copy-start(bf16[2,2048,128]{2,1,0:T(8,128)(2,1)} %param.24) | copy-start | bytes 3145732
  25.7 35.4 %copy-start = (bf16[2,256,2048]{2,1,0:T(8,128)(2,1)S(1)}, bf16[2,256,2048]{2,1,0:T(8,128)(2,1)}, u32[]{:S(2)}) copy-start(bf16[2,256,2048]{2,1,0:T(8,128)(2,1)} %param.25) | copy-start | bytes 6291460
  29.3 3.7 %collective-permute-start.5 = (f32[2,1,2]{2,0,1:T(2,128)S(1)}, f32[2,1,2]{2,0,1:T(2,128)S(1)}, u32[]{:S(2)}, u32[]{:S(2)}) collective-permute-start(f32[2,1,2]{2,0,1:T(2,128)S(1)} %bitcast.429), channel_id=1, source_target_pairs={{0,8},{8,0},{16,24},{24,16},{32,40},{40,32},{48,56},{56,48},{64,72... | collective-permute-start | bytes 56 | tf_op jit(solution)/shard_map/ppermute | solution.py:20
  29.5 3.6 %collective-permute-start.3 = (f32[2,1,2]{2,0,1:T(2,128)S(1)}, f32[2,1,2]{2,0,1:T(2,128)S(1)}, u32[]{:S(2)}, u32[]{:S(2)}) collective-permute-start(f32[2,1,2]{2,0,1:T(2,128)S(1)} %bitcast.428), channel_id=1, source_target_pairs={{0,8},{8,0},{16,24},{24,16},{32,40},{40,32},{48,56},{56,48},{64,72... | collective-permute-start | bytes 56 | tf_op jit(solution)/shard_map/ppermute | solution.py:20
  31.4 3.6 %collective-permute-start.4 = (f32[2,1,2,128]{3,2,0,1:T(2,128)S(1)}, f32[2,1,2,128]{3,2,0,1:T(2,128)S(1)}, u32[]{:S(2)}, u32[]{:S(2)}) collective-permute-start(f32[2,1,2,128]{3,2,0,1:T(2,128)S(1)} %bitcast.435), channel_id=1, source_target_pairs={{0,8},{8,0},{16,24},{24,16},{32,40},{40,32},{48,56},{56,48},{64,72... | collective-permute-start | bytes 6152 | tf_op jit(solution)/shard_map/ppermute | solution.py:20
  86.5 7.4 %copy-start.7 = (bf16[2,2,1,2,2048,1,128]{6,4,5,3,2,1,0:T(8,128)(2,1)S(1)}, bf16[2,2,1,2,2048,1,128]{6,4,5,3,2,1,0:T(8,128)(2,1)}, u32[]{:S(2)}) copy-start(bf16[2,2,1,2,2048,1,128]{6,4,5,3,2,1,0:T(8,128)(2,1)} %param.16) | copy-start | bytes 12582916
  103.2 3.7 %collective-permute-start.8 = (f32[2,1,2]{2,0,1:T(2,128)S(1)}, f32[2,1,2]{2,0,1:T(2,128)S(1)}, u32[]{:S(2)}, u32[]{:S(2)}) collective-permute-start(f32[2,1,2]{2,0,1:T(2,128)S(1)} %bitcast.427), channel_id=1, source_target_pairs={{0,8},{8,0},{16,24},{24,16},{32,40},{40,32},{48,56},{56,48},{64,72... | collective-permute-start | bytes 56 | tf_op jit(solution)/shard_map/ppermute | solution.py:20
  103.7 3.6 %collective-permute-start.6 = (f32[2,1,2]{2,0,1:T(2,128)S(1)}, f32[2,1,2]{2,0,1:T(2,128)S(1)}, u32[]{:S(2)}, u32[]{:S(2)}) collective-permute-start(f32[2,1,2]{2,0,1:T(2,128)S(1)} %bitcast.426), channel_id=1, source_target_pairs={{0,8},{8,0},{16,24},{24,16},{32,40},{40,32},{48,56},{56,48},{64,72... | collective-permute-start | bytes 56 | tf_op jit(solution)/shard_map/ppermute | solution.py:20
  105.3 3.6 %collective-permute-start.7 = (f32[2,1,2,128]{3,2,0,1:T(2,128)S(1)}, f32[2,1,2,128]{3,2,0,1:T(2,128)S(1)}, u32[]{:S(2)}, u32[]{:S(2)}) collective-permute-start(f32[2,1,2,128]{3,2,0,1:T(2,128)S(1)} %bitcast.434), channel_id=1, source_target_pairs={{0,8},{8,0},{16,24},{24,16},{32,40},{40,32},{48,56},{56,48},{64,72... | collective-permute-start | bytes 6152 | tf_op jit(solution)/shard_map/ppermute | solution.py:20
where the time goes:
time: 138 us
  blocking collectives  48.8 us (35%)
  waiting for transfers between devices  28.8 us (21%)
  matrix products  27.8 us (20%)
  local copies, waits for them, and re-layouts  13.2 us (10%)
  starting transfers between devices  10.3 us (7%)
  other arithmetic  5.61 us (4%)
  between operations  3.04 us (2%)
    psum x2, blocking collectives, local(): summed = lax.psum(heads_out, 'tensor')  48.8 us
    ppermute x2, waiting for transfers between devices, shifted(): return lax.ppermute(block, axis, route)  23.1 us
    dot_general x6, matrix products, masked_scores(): jnp.einsum('kgd,tkd->kgt', grouped, key_rows, preferred_element_type=jnp....  8.49 us
    ppermute x7, starting transfers between devices, partner_2(): return lax.ppermute(value, axis, pairs)  6.68 us
    ppermute x7, waiting for transfers between devices, partner_2(): return lax.ppermute(value, axis, pairs)  5.76 us
    dot_general x4, matrix products, attend(): jnp.einsum('kgt,tkd->kgd', weights.astype(jnp.bfloat16), value_rows, pref...  5.64 us
    dot_general x4, matrix products, project(): jnp.dot(normed, key_weight, preferred_element_type=jnp.float32)  5.57 us
    ppermute x2, starting transfers between devices, shifted(): return lax.ppermute(block, axis, route)  3.62 us
  transfers between devices with their start and end apart: 9, of which 7 were waited for; matrix products, arithmetic and copies ran while one was open for 15% of the time, Pallas kernels for 0%

commit v1 on v0

--- a/solution.py
+++ b/solution.py
@@ -6,6 +6,12 @@
 EPSILON = 1e-06
 ROPE_BASE = 1000000.0
 NEGATIVE = -1e30
+
+
+def add_all(shard, mesh_axis):
+    parts = lax.all_gather(shard, mesh_axis, axis=0, tiled=False)
+    total = parts.sum(axis=0)
+    return total
 
 
 def shifted(block, axis, distance):
@@ -224,7 +230,7 @@
             w_out[layer_at],
             preferred_element_type=jnp.float32,
         )
-        summed = lax.psum(heads_out, "tensor")
+        summed = add_all(heads_out, "tensor")
         carried = jnp.concatenate([hidden, long_hidden], axis=0).astype(jnp.float32) + summed
         if layer_at + 1 < layers:
             carried = carried.astype(jnp.bfloat16)

time: 138 us -> 120 us (0.87); the launches traced: 138 us -> 118 us
  blocking collectives: 48.8 us -> 27.8 us
    psum x2 -> x0, blocking collectives: 48.8 us -> none  [local(): summed = lax.psum(heads_out, 'tensor')]
    all_gather x0 -> x2, blocking collectives: none -> 27.8 us  [add_all(): parts = lax.all_gather(shard, mesh_axis, axis=0, tiled=False)]
  transfers between devices with their start and end apart: 9 -> 9, of which waited for: 7 -> 7; matrix products, arithmetic and copies ran while one was open for 15% -> 18% of each run, Pallas kernels for 0% -> 0%
where the time goes in v1:
time: 120 us; the launch traced here: 118 us
  waiting for transfers between devices  29 us (24%)
  matrix products  27.8 us (23%)
  blocking collectives  27.8 us (23%)
  local copies, waits for them, and re-layouts  13.2 us (11%)
  starting transfers between devices  10.1 us (8%)
  other arithmetic  6.74 us (6%)
  between operations  3.03 us (3%)
    all_gather x2, blocking collectives, add_all(): parts = lax.all_gather(shard, mesh_axis, axis=0, tiled=False)  27.8 us
    ppermute x2, waiting for transfers between devices, shifted(): return lax.ppermute(block, axis, route)  23.1 us
    dot_general x6, matrix products, masked_scores(): jnp.einsum('kgd,tkd->kgt', grouped, key_rows, preferred_element_type=jnp....  8.49 us
    ppermute x7, starting transfers between devices, partner_2(): return lax.ppermute(value, axis, pairs)  6.51 us
    ppermute x7, waiting for transfers between devices, partner_2(): return lax.ppermute(value, axis, pairs)  5.93 us
    dot_general x4, matrix products, attend(): jnp.einsum('kgt,tkd->kgd', weights.astype(jnp.bfloat16), value_rows, pref...  5.64 us
    dot_general x4, matrix products, project(): jnp.dot(normed, key_weight, preferred_element_type=jnp.float32)  5.57 us
    ppermute x2, starting transfers between devices, shifted(): return lax.ppermute(block, axis, route)  3.62 us
  transfers between devices with their start and end apart: 9, of which 7 were waited for; matrix products, arithmetic and copies ran while one was open for 18% of the time, Pallas kernels for 0%

profile of v1, /device:TPU:64, one launch (start us, length us, event | category | flops | bytes accessed | tf_op | source)
XLA Modules:
  0.0 117.7 jit_solution(5312890221545724412)
XLA Ops:
  0.6 0.7 slice.220
  1.4 3.1 %collective-permute-start = (bf16[1,2048]{1,0:T(2,128)(2,1)S(1)}, bf16[1,2048]{1,0:T(2,128)(2,1)S(1)}, u32[]{:S(2)}, u32[]{:S(2)}) collective-permute-start(bf16[1,2048]{1,0:T(2,128)(2,1)S(1)} %slice.220), channel_id=1, source_target_pairs={{128,0},{136,8},{144,16},{152,24},{160,32},{168,40},{176,48},{184,... | collective-permute-start | bytes 12296 | tf_op jit(solution)/shard_map/ppermute | solution.py:20
  4.5 1.9 %collective-permute-start.1 = (bf16[1,2048]{1,0:T(2,128)(2,1)}, bf16[1,2048]{1,0:T(2,128)(2,1)S(1)}, u32[]{:S(2)}, u32[]{:S(2)}) collective-permute-start(bf16[1,2048]{1,0:T(2,128)(2,1)} %param.14), channel_id=1, source_target_pairs={{0,8},{8,0},{16,24},{24,16},{32,40},{40,32},{48,56},{56,48},{64,72... | collective-permute-start | bytes 12296 | tf_op jit(solution)/shard_map/ppermute | solution.py:26
  6.5 3.0 %slice_bitcast_fusion = bf16[2,2,2048,1,128]{4,2,1,0,3:T(8,128)(2,1)} fusion(bf16[2,2,3,2048,1,128]{5,3,4,2,1,0:T(8,128)(2,1)} %param.15), kind=kLoop, calls=%fused_computation.14 | loop fusion | bytes 4194304 | tf_op jit(solution)/shard_map/squeeze | solution.py:164
  9.5 0.5 collective-permute-start.2
  10.0 0.6 dynamic_slice.14
  10.7 0.7 fusion.198
  11.9 1.7 %slice_bitcast_fusion.18 = (bf16[256,2048]{0,1:T(8,128)(2,1)S(1)}, bf16[256,2048]{0,1:T(8,128)(2,1)S(1)}) fusion(bf16[2,2048,256]{2,1,0:T(8,128)(2,1)} %param.22), kind=kLoop, calls=%fused_computation.56 | loop fusion | bytes 4194304 | tf_op jit(solution)/shard_map/dot_general | solution.py:53
  15.0 0.6 copy.52
  15.7 0.6 copy.60
  17.2 1.4 %multiply_reduce_fusion.5 = (f32[3]{0:T(128)S(1)}, f32[3,128]{1,0:T(4,128)S(1)}) fusion(bf16[2,2048,128]{2,1,0:T(8,128)(2,1)} %param.23, f32[2048]{0:T(1024)S(1)} %bitcast.418, f32[3]{0:T(128)S(1)} %add_rsqrt_fusion.11, bf16[1,2048]{1,0:T(2,128)(2,1)S(1)} %collective-permute-done, bf16[2,2048]{1,0:T(2,128)(2,1)S(1)} %slice.219), kind=kOutput, calls=%fused_computation.200 | convolution fusion | flops 1616637 | bytes 546328 | tf_op jit(solution)/shard_map/dot_general | solution.py:56
  19.0 1.4 %multiply_reduce_fusion.7 = (f32[2]{0:T(128)S(1)}, f32[2,128]{1,0:T(2,128)S(1)}) fusion(bf16[2,2048,128]{2,1,0:T(8,128)(2,1)} %param.23, bf16[2,2048]{1,0:T(2,128)(2,1)S(1)} %get-tuple-element.12, f32[2]{0:T(128)S(1)} %add_rsqrt_fusion.9, f32[2048]{0:T(1024)S(1)} %bitcast.419), kind=kOutput, calls=%fused_computation.252 | convolution fusion | flops 1065470 | bytes 541712 | tf_op jit(solution)/shard_map/dot_general | solution.py:56
  20.4 0.5 multiply_reduce_fusion.4
  21.1 1.7 %fusion.201 = (f32[2,2]{1,0:T(2,128)S(1)}, f32[2,2,2048]{2,1,0:T(2,128)S(1)}) fusion(bf16[2,2,1,2,2048,1,128]{6,4,3,5,2,1,0:T(8,128)(2,1)} %bitcast.445, bf16[2,2,128]{2,0,1:T(2,128)(2,1)S(1)} %pad_maximum_fusion.4, pred[2,2048]{1,0:T(4,128)(4,1)S(1)} %broadcast_compare_fusion), kind=kOutput, calls=%fused_computation.350 | convolution fusion | flops 2121724 | bytes 1086480 | tf_op jit(solution)/shard_map/vmap(kgd,tkd->kgt)/dot_general | solution.py:80
  23.0 1.5 %fusion.23 = f32[2,2,128]{2,1,0:T(2,128)S(1)} fusion(bf16[2,2,1,2,2048,1,128]{6,4,3,5,2,1,0:T(8,128)(2,1)} %bitcast.446, f32[2,2,2048]{2,1,0:T(2,128)S(1)} %get-tuple-element.64, f32[2,2]{1,0:T(2,128)S(1)} %get-tuple-element.63), kind=kOutput, calls=%fused_computation.47 | convolution fusion | flops 2113536 | bytes 1083408 | tf_op jit(solution)/shard_map/vmap(kgt,tkd->kgd)/dot_general | solution.py:105
  24.8 0.5 multiply_reduce_fusion.1
  25.7 1.8 %fusion.203 = (f32[2,2]{1,0:T(2,128)S(1)}, f32[2,2,2048]{2,1,0:T(2,128)S(1)}) fusion(bf16[2,2,3,2048,1,128]{5,3,2,4,1,0:T(8,128)(2,1)} %bitcast.408, bf16[2,2,128]{2,0,1:T(2,128)(2,1)S(1)} %fusion.141, pred[2,2048]{1,0:T(4,128)(4,1)S(1)} %bitcast.424), kind=kOutput, calls=%fused_computation.352 | convolution fusion | flops 2121724 | bytes 1086480 | tf_op jit(solution)/shard_map/vmap(kgd,tkd->kgt)/dot_general | solution.py:80
  27.7 1.5 %fusion.11 = bf16[1,2,2,128]{3,2,1,0:T(2,128)(2,1)S(1)} fusion(bf16[2,2,3,2048,1,128]{5,3,2,4,1,0:T(8,128)(2,1)} %bitcast.409, f32[2,2,2048]{2,1,0:T(2,128)S(1)} %get-tuple-element.72, f32[2,2]{1,0:T(2,128)S(1)} %multiply_maximum_fusion.1, f32[2,2]{1,0:T(2,128)S(1)} %get-tuple-element.42, f32[2,128]{1,0:T(2,128)S(1)} %slice_convert_fusion.1, ...), kind=kOutput, calls=%fused_computation.24 | convolution fusion | flops 2115584 | bytes 1083440 | tf_op jit(solution)/shard_map/vmap(kgt,tkd->kgd)/dot_general | solution.py:93
  29.5 1.9 %collective-permute-start.3 = (f32[2,1,2]{2,0,1:T(2,128)S(1)}, f32[2,1,2]{2,0,1:T(2,128)S(1)}, u32[]{:S(2)}, u32[]{:S(2)}) collective-permute-start(f32[2,1,2]{2,0,1:T(2,128)S(1)} %bitcast.432), channel_id=1, source_target_pairs={{0,8},{8,0},{16,24},{24,16},{32,40},{40,32},{48,56},{56,48},{64,72... | collective-permute-start | bytes 56 | tf_op jit(solution)/shard_map/ppermute | solution.py:26
  32.3 0.6 collective-permute-done.5
  33.1 1.9 %collective-permute-done.4 = f32[2,1,2,128]{3,2,0,1:T(2,128)S(1)} collective-permute-done((f32[2,1,2,128]{3,2,0,1:T(2,128)S(1)}, f32[2,1,2,128]{3,2,0,1:T(2,128)S(1)}, u32[]{:S(2)}, u32[]{:S(2)}) %collective-permute-start.4) | collective-permute-done | bytes 2080 | tf_op jit(solution)/shard_map/ppermute | solution.py:26
  35.1 23.0 %collective-permute-done.2 = bf16[2,2,2048,1,128]{4,2,1,0,3:T(8,128)(2,1)} collective-permute-done((bf16[2,2,2048,1,128]{4,2,1,0,3:T(8,128)(2,1)}, bf16[2,2,2048,1,128]{4,2,1,0,3:T(8,128)(2,1)}, u32[]{:S(2)}, u32[]{:S(2)}) %collective-permute-start.2) | collective-permute-done | bytes 2097184 | tf_op jit(solution)/shard_map/ppermute | solution.py:20
  58.1 1.4 %fusion.202 = (f32[2]{0:T(128)S(1)}, f32[2,2048]{1,0:T(2,128)S(1)}) fusion(bf16[2,2,2048,1,128]{4,2,1,0,3:T(8,128)(2,1)} %collective-permute-done.2, bf16[1,2,128]{2,0,1:T(2,128)(2,1)S(1)} %pad_maximum_fusion.2, pred[2048]{0:T(1024)(128)(4,1)S(1)} %slice_reduce_fusion), kind=kOutput, calls=%fused_computation.351 | convolution fusion | flops 1060862 | bytes 543240 | tf_op jit(solution)/shard_map/kgd,tkd->kgt/dot_general | solution.py:80
  59.8 1.3 %fusion.19 = bf16[1,1,2,128]{3,2,1,0:T(2,128)(2,1)S(1)} fusion(bf16[2,2,2048,1,128]{4,2,1,0,3:T(8,128)(2,1)} %collective-permute-done.2, f32[2,2048]{1,0:T(2,128)S(1)} %get-tuple-element.70, f32[2]{0:T(128)S(1)} %get-tuple-element.6, f32[2]{0:T(128)S(1)} %fusion.182, f32[128]{0:T(128)S(1)} %get-tuple-element.48, f32[2]{0:T(128)S(1)} %bitcast_convert_fusion.6), kind=kOutput, calls=%fused_computation.36 | convolution fusion | flops 1057792 | bytes 541720 | tf_op jit(solution)/shard_map/kgt,tkd->kgd/dot_general | solution.py:93
  61.3 14.7 %all-gather.2 = f32[8,5,2048]{2,1,0:T(8,128)} all-gather(f32[1,5,2048]{2,1,0:T(8,128)S(1)} %convolution_bitcast_fusion.1), channel_id=2, replica_groups=mesh['replica'=32,'tensor'=8] {'tensor'}, dimensions={0}, use_global_device_ids=true | all-gather | bytes 368640 | tf_op jit(solution)/shard_map/all_gather | solution.py:12
  76.0 1.1 reduce_sum.194
  77.4 1.4 %convolution_convert_fusion = bf16[3,128]{1,0:T(4,128)(2,1)S(1)} fusion(bf16[2,2048,128]{2,1,0:T(8,128)(2,1)} %param.24, f32[2048]{0:T(1024)S(1)} %bitcast.412, f32[3]{0:T(128)S(1)} %add_rsqrt_fusion.7, bf16[5,2048]{1,0:T(8,128)(2,1)S(1)} %add_convert_fusion), kind=kOutput, calls=%fused_computation.19 | convolution fusion | flops 1597824 | bytes 550144 | tf_op jit(solution)/shard_map/dot_general | solution.py:60
  78.9 1.3 %fusion.16 = f32[2,128]{1,0:T(2,128)S(1)} fusion(bf16[2,2048,128]{2,1,0:T(8,128)(2,1)} %param.24, f32[2]{0:T(128)S(1)} %add_rsqrt_fusion.5, f32[2048]{0:T(1024)S(1)} %bitcast.413, bf16[5,2048]{1,0:T(8,128)(2,1)S(1)} %add_convert_fusion), kind=kOutput, calls=%fused_computation.32 | convolution fusion | flops 1065472 | bytes 542208 | tf_op jit(solution)/shard_map/dot_general | solution.py:60
  80.2 1.4 %multiply_reduce_fusion.6 = (f32[2]{0:T(128)S(1)}, f32[2,128]{1,0:T(2,128)S(1)}) fusion(bf16[2,2048,128]{2,1,0:T(8,128)(2,1)} %param.23, f32[2]{0:T(128)S(1)} %add_rsqrt_fusion.5, f32[2048]{0:T(1024)S(1)} %bitcast.414, bf16[5,2048]{1,0:T(8,128)(2,1)S(1)} %add_convert_fusion), kind=kOutput, calls=%fused_computation.244 | convolution fusion | flops 1065470 | bytes 542216 | tf_op jit(solution)/shard_map/dot_general | solution.py:56
  81.6 0.5 multiply_reduce_fusion.2
  82.0 0.5 multiply_reduce_fusion
  82.5 1.4 %multiply_reduce_fusion.3 = (f32[3]{0:T(128)S(1)}, f32[3,128]{1,0:T(4,128)S(1)}) fusion(bf16[2,2048,128]{2,1,0:T(8,128)(2,1)} %param.23, f32[2048]{0:T(1024)S(1)} %bitcast.417, f32[3]{0:T(128)S(1)} %add_rsqrt_fusion.7, bf16[5,2048]{1,0:T(8,128)(2,1)S(1)} %add_convert_fusion), kind=kOutput, calls=%fused_computation.194 | convolution fusion | flops 1598205 | bytes 550924 | tf_op jit(solution)/shard_map/dot_general | solution.py:56
  84.8 0.5 fusion.204
  85.4 0.3 fusion.22
  86.3 1.7 %fusion.206 = (f32[2,2]{1,0:T(2,128)S(1)}, f32[2,2,2048]{2,1,0:T(2,128)S(1)}) fusion(bf16[2,2,3,2048,1,128]{5,3,2,4,1,0:T(8,128)(2,1)} %bitcast.410, bf16[2,2,128]{2,0,1:T(2,128)(2,1)S(1)} %fusion.140, pred[2,2048]{1,0:T(4,128)(4,1)S(1)} %bitcast.425), kind=kOutput, calls=%fused_computation.355 | convolution fusion | flops 2121724 | bytes 1086480 | tf_op jit(solution)/shard_map/vmap(kgd,tkd->kgt)/dot_general | solution.py:80
  88.1 1.4 %fusion.205 = (f32[2]{0:T(128)S(1)}, f32[2,2048]{1,0:T(2,128)S(1)}) fusion(bf16[2,2,2048,1,128]{4,2,1,0,3:T(8,128)(2,1)} %collective-permute-done.2, bf16[1,2,128]{2,0,1:T(2,128)(2,1)S(1)} %pad_maximum_fusion.1, pred[2048]{0:T(1024)(128)(4,1)S(1)} %slice_reduce_fusion), kind=kOutput, calls=%fused_computation.354 | convolution fusion | flops 1060862 | bytes 543240 | tf_op jit(solution)/shard_map/kgd,tkd->kgt/dot_general | solution.py:80
  89.8 1.3 %fusion.18 = bf16[1,1,2,128]{3,2,1,0:T(2,128)(2,1)S(1)} fusion(bf16[2,2,2048,1,128]{4,2,1,0,3:T(8,128)(2,1)} %collective-permute-done.2, f32[2,2048]{1,0:T(2,128)S(1)} %get-tuple-element.84, f32[2]{0:T(128)S(1)} %get-tuple-element.4, f32[2]{0:T(128)S(1)} %fusion.183, f32[128]{0:T(128)S(1)} %get-tuple-element.50, f32[2]{0:T(128)S(1)} %bitcast_convert_fusion.2), kind=kOutput, calls=%fused_computation.35 | convolution fusion | flops 1057792 | bytes 541720 | tf_op jit(solution)/shard_map/kgt,tkd->kgd/dot_general | solution.py:93
  91.1 1.3 %dynamic_update_slice.4 = bf16[1,2,2,2048,1,128]{5,3,4,2,1,0:T(8,128)(2,1)} dynamic-update-slice(bf16[1,2,2,2048,1,128]{5,3,4,2,1,0:T(8,128)(2,1)} %bitcast.103, bf16[1,2,2,1,1,128]{5,3,4,2,1,0:T(2,128)(2,1)S(1)} %copy.69, s32[]{:T(128)} %constant.71.clone.1, s32[]{:T(128)} %constant.71.clone.1, s32[]{:T(128)} %constant.71.clone.1, s32[]{:T(128)S(6)} %select_n.75, s32[]{:T(128)} %constant.71.clone.1, ...) | dynamic-update-slice | bytes 2052 | tf_op jit(solution)/shard_map/dynamic_update_slice | solution.py:240
  92.6 1.5 %fusion.10 = bf16[1,2,2,128]{3,2,1,0:T(2,128)(2,1)S(1)} fusion(bf16[2,2,3,2048,1,128]{5,3,2,4,1,0:T(8,128)(2,1)} %bitcast.411, f32[2,2,2048]{2,1,0:T(2,128)S(1)} %get-tuple-element.86, f32[2,2]{1,0:T(2,128)S(1)} %multiply_maximum_fusion, f32[2,2]{1,0:T(2,128)S(1)} %get-tuple-element.36, f32[2,128]{1,0:T(2,128)S(1)} %slice_convert_fusion, ...), kind=kOutput, calls=%fused_computation.23 | convolution fusion | flops 2115584 | bytes 1083440 | tf_op jit(solution)/shard_map/vmap(kgt,tkd->kgd)/dot_general | solution.py:93
  94.2 0.3 collective-permute-start.8
  94.5 1.8 %collective-permute-start.6 = (f32[2,1,2]{2,0,1:T(2,128)S(1)}, f32[2,1,2]{2,0,1:T(2,128)S(1)}, u32[]{:S(2)}, u32[]{:S(2)}) collective-permute-start(f32[2,1,2]{2,0,1:T(2,128)S(1)} %bitcast.430), channel_id=1, source_target_pairs={{0,8},{8,0},{16,24},{24,16},{32,40},{40,32},{48,56},{56,48},{64,72... | collective-permute-start | bytes 56 | tf_op jit(solution)/shard_map/ppermute | solution.py:26
  96.3 0.3 collective-permute-start.7
  96.5 1.3 %collective-permute-done.8 = f32[2,1,2]{2,0,1:T(2,128)S(1)} collective-permute-done((f32[2,1,2]{2,0,1:T(2,128)S(1)}, f32[2,1,2]{2,0,1:T(2,128)S(1)}, u32[]{:S(2)}, u32[]{:S(2)}) %collective-permute-start.8) | collective-permute-done | bytes 48 | tf_op jit(solution)/shard_map/ppermute | solution.py:26
  98.1 1.8 %collective-permute-done.7 = f32[2,1,2,128]{3,2,0,1:T(2,128)S(1)} collective-permute-done((f32[2,1,2,128]{3,2,0,1:T(2,128)S(1)}, f32[2,1,2,128]{3,2,0,1:T(2,128)S(1)}, u32[]{:S(2)}, u32[]{:S(2)}) %collective-permute-start.7) | collective-permute-done | bytes 2080 | tf_op jit(solution)/shard_map/ppermute | solution.py:26
  100.2 13.1 %all-gather.3 = f32[8,5,2048]{2,1,0:T(8,128)S(1)} all-gather(f32[1,5,2048]{2,1,0:T(8,128)S(1)} %convolution_bitcast_fusion), channel_id=3, replica_groups=mesh['replica'=32,'tensor'=8] {'tensor'}, dimensions={0}, use_global_device_ids=true | all-gather | bytes 368640 | tf_op jit(solution)/shard_map/all_gather | solution.py:12
  113.4 0.6 slice.313
  114.0 0.6 constant_dynamic-slice_fusion
  114.6 3.0 %copy.143 = bf16[1,2,2,2048,1,128]{5,3,4,2,1,0:T(8,128)(2,1)} copy(bf16[1,2,2,2048,1,128]{5,3,4,2,1,0:T(8,128)(2,1)} %dynamic_update_slice.4) | data formatting | bytes 4194304
  (136 shorter events, 7.6 us)
Async XLA Ops:
  1.4 8.7 %copy-start.9 = (s32[96]{0:T(128)S(1)}, s32[96]{0:T(128)}, u32[]{:S(2)}) copy-start(s32[96]{0:T(128)} %param.17) | copy-start | bytes 1156
  1.4 9.3 %copy-start.4 = (f32[2,128]{1,0:T(2,128)S(1)}, f32[2,128]{1,0:T(2,128)}, u32[]{:S(2)}) copy-start(f32[2,128]{1,0:T(2,128)} %param.20) | copy-start | bytes 3076
  1.4 9.3 %copy-start.5 = (f32[2,128]{1,0:T(2,128)S(1)}, f32[2,128]{1,0:T(2,128)}, u32[]{:S(2)}) copy-start(f32[2,128]{1,0:T(2,128)} %param.21) | copy-start | bytes 3076
  1.4 10.0 %copy-start.6 = (s32[32]{0:T(128)S(1)}, s32[32]{0:T(128)}, u32[]{:S(2)}) copy-start(s32[32]{0:T(128)} %param.18) | copy-start | bytes 388
  1.4 10.4 %copy-start.1 = (f32[2,2048]{1,0:T(2,128)S(1)}, f32[2,2048]{1,0:T(2,128)}, u32[]{:S(2)}) copy-start(f32[2,2048]{1,0:T(2,128)} %param.19) | copy-start | bytes 49156
  1.4 15.6 %collective-permute-start = (bf16[1,2048]{1,0:T(2,128)(2,1)S(1)}, bf16[1,2048]{1,0:T(2,128)(2,1)S(1)}, u32[]{:S(2)}, u32[]{:S(2)}) collective-permute-start(bf16[1,2048]{1,0:T(2,128)(2,1)S(1)} %slice.220), channel_id=1, source_target_pairs={{128,0},{136,8},{144,16},{152,24},{160,32},{168,40},{176,48},{184,... | collective-permute-start | bytes 12296 | tf_op jit(solution)/shard_map/ppermute | solution.py:20
  4.5 14.3 %collective-permute-start.1 = (bf16[1,2048]{1,0:T(2,128)(2,1)}, bf16[1,2048]{1,0:T(2,128)(2,1)S(1)}, u32[]{:S(2)}, u32[]{:S(2)}) collective-permute-start(bf16[1,2048]{1,0:T(2,128)(2,1)} %param.14), channel_id=1, source_target_pairs={{0,8},{8,0},{16,24},{24,16},{32,40},{40,32},{48,56},{56,48},{64,72... | collective-permute-start | bytes 12296 | tf_op jit(solution)/shard_map/ppermute | solution.py:26
  9.5 48.6 %collective-permute-start.2 = (bf16[2,2,2048,1,128]{4,2,1,0,3:T(8,128)(2,1)}, bf16[2,2,2048,1,128]{4,2,1,0,3:T(8,128)(2,1)}, u32[]{:S(2)}, u32[]{:S(2)}) collective-permute-start(bf16[2,2,2048,1,128]{4,2,1,0,3:T(8,128)(2,1)} %slice_bitcast_fusion), channel_id=1, source_target_pairs={{128,0},{136,8},{144,16},{152,24},{160,32},{168,40},{176,48},{184,... | collective-permute-start | bytes 6291464 | tf_op jit(solution)/shard_map/ppermute | solution.py:20
  11.9 3.1 %copy-start.2 = (bf16[3,2048]{1,0:T(4,128)(2,1)S(1)}, bf16[3,2048]{1,0:T(4,128)(2,1)}, u32[]{:S(2)}) copy-start(bf16[3,2048]{1,0:T(4,128)(2,1)} %param.13) | copy-start | bytes 36868
  15.0 3.8 %copy-start.3 = (bf16[1,2048]{1,0:T(2,128)(2,1)S(1)}, bf16[1,2048]{1,0:T(2,128)(2,1)}, u32[]{:S(2)}) copy-start(bf16[1,2048]{1,0:T(2,128)(2,1)} %param.14) | copy-start | bytes 12292
  18.5 6.0 %copy-start.8 = (bf16[2,2048,128]{2,1,0:T(8,128)(2,1)S(1)}, bf16[2,2048,128]{2,1,0:T(8,128)(2,1)}, u32[]{:S(2)}) copy-start(bf16[2,2048,128]{2,1,0:T(8,128)(2,1)} %param.24) | copy-start | bytes 3145732
  25.7 35.4 %copy-start = (bf16[2,256,2048]{2,1,0:T(8,128)(2,1)S(1)}, bf16[2,256,2048]{2,1,0:T(8,128)(2,1)}, u32[]{:S(2)}) copy-start(bf16[2,256,2048]{2,1,0:T(8,128)(2,1)} %param.25) | copy-start | bytes 6291460
  29.3 3.7 %collective-permute-start.5 = (f32[2,1,2]{2,0,1:T(2,128)S(1)}, f32[2,1,2]{2,0,1:T(2,128)S(1)}, u32[]{:S(2)}, u32[]{:S(2)}) collective-permute-start(f32[2,1,2]{2,0,1:T(2,128)S(1)} %bitcast.433), channel_id=1, source_target_pairs={{0,8},{8,0},{16,24},{24,16},{32,40},{40,32},{48,56},{56,48},{64,72... | collective-permute-start | bytes 56 | tf_op jit(solution)/shard_map/ppermute | solution.py:26
  29.5 3.6 %collective-permute-start.3 = (f32[2,1,2]{2,0,1:T(2,128)S(1)}, f32[2,1,2]{2,0,1:T(2,128)S(1)}, u32[]{:S(2)}, u32[]{:S(2)}) collective-permute-start(f32[2,1,2]{2,0,1:T(2,128)S(1)} %bitcast.432), channel_id=1, source_target_pairs={{0,8},{8,0},{16,24},{24,16},{32,40},{40,32},{48,56},{56,48},{64,72... | collective-permute-start | bytes 56 | tf_op jit(solution)/shard_map/ppermute | solution.py:26
  31.4 3.6 %collective-permute-start.4 = (f32[2,1,2,128]{3,2,0,1:T(2,128)S(1)}, f32[2,1,2,128]{3,2,0,1:T(2,128)S(1)}, u32[]{:S(2)}, u32[]{:S(2)}) collective-permute-start(f32[2,1,2,128]{3,2,0,1:T(2,128)S(1)} %bitcast.439), channel_id=1, source_target_pairs={{0,8},{8,0},{16,24},{24,16},{32,40},{40,32},{48,56},{56,48},{64,72... | collective-permute-start | bytes 6152 | tf_op jit(solution)/shard_map/ppermute | solution.py:26
  77.4 7.4 %copy-start.7 = (bf16[2,2,1,2,2048,1,128]{6,4,5,3,2,1,0:T(8,128)(2,1)S(1)}, bf16[2,2,1,2,2048,1,128]{6,4,5,3,2,1,0:T(8,128)(2,1)}, u32[]{:S(2)}) copy-start(bf16[2,2,1,2,2048,1,128]{6,4,5,3,2,1,0:T(8,128)(2,1)} %param.16) | copy-start | bytes 12582916
  94.2 3.7 %collective-permute-start.8 = (f32[2,1,2]{2,0,1:T(2,128)S(1)}, f32[2,1,2]{2,0,1:T(2,128)S(1)}, u32[]{:S(2)}, u32[]{:S(2)}) collective-permute-start(f32[2,1,2]{2,0,1:T(2,128)S(1)} %bitcast.431), channel_id=1, source_target_pairs={{0,8},{8,0},{16,24},{24,16},{32,40},{40,32},{48,56},{56,48},{64,72... | collective-permute-start | bytes 56 | tf_op jit(solution)/shard_map/ppermute | solution.py:26
  94.5 3.6 %collective-permute-start.6 = (f32[2,1,2]{2,0,1:T(2,128)S(1)}, f32[2,1,2]{2,0,1:T(2,128)S(1)}, u32[]{:S(2)}, u32[]{:S(2)}) collective-permute-start(f32[2,1,2]{2,0,1:T(2,128)S(1)} %bitcast.430), channel_id=1, source_target_pairs={{0,8},{8,0},{16,24},{24,16},{32,40},{40,32},{48,56},{56,48},{64,72... | collective-permute-start | bytes 56 | tf_op jit(solution)/shard_map/ppermute | solution.py:26
  96.3 3.6 %collective-permute-start.7 = (f32[2,1,2,128]{3,2,0,1:T(2,128)S(1)}, f32[2,1,2,128]{3,2,0,1:T(2,128)S(1)}, u32[]{:S(2)}, u32[]{:S(2)}) collective-permute-start(f32[2,1,2,128]{3,2,0,1:T(2,128)S(1)} %bitcast.438), channel_id=1, source_target_pairs={{0,8},{8,0},{16,24},{24,16},{32,40},{40,32},{48,56},{56,48},{64,72... | collective-permute-start | bytes 6152 | tf_op jit(solution)/shard_map/ppermute | solution.py:26
